TPU v7x, 32 devices: a whole 2x2x4 slice. The times are simulated.
32 devices in a mesh: section: 4 (over z), tp: 8 (over y, x, core).
Axes of the slice: x: 2, y: 2, z: 4, core: 2. Of those that a mesh axis runs over, the one named last changes fastest.
Arguments:
- hidden_entering: bfloat16 [4, 16, 8192], P('section', None, 'tp'), may hold values from -6 to 6
- layer_norm_gain: bfloat16 [4, 8192], P('section'), may hold values from 0.25 to 1.75
- query_matrix: bfloat16 [4, 8192, 4096], P('section', None, 'tp'), may hold values from -0.0625 to 0.0625
- output_matrix: bfloat16 [4, 4096, 8192], P('section', 'tp'), may hold values from -0.09375 to 0.09375
- adapter_down_weight: bfloat16 [4, 4, 64, 8192], P('section', None, 'tp'), may hold values from -0.0625 to 0.0625
- adapter_up_weight: bfloat16 [4, 4, 64, 4096], P('section', None, None, 'tp'), may hold values from -0.75 to 0.75
- key_value_cache: bfloat16 [4, 3, 16, 32, 1024], P('section', None, 'tp')
- adapter_index: int32 [4, 16], replicated, may hold values from 0 to 3
- cached_lengths: int32 [4, 16], replicated, may hold values from 1 to 32, as said below
Outputs:
- section_out: bfloat16 [4, 3, 16, 8192], P('section', None, None, 'tp')
Inputs may be any that keep to these rules, and one draw needn't show every extreme that they name: `cached_lengths`: in every group some request uses all 32 cached positions.
All inputs are finite; a program needn't handle non-finite values.
Results may differ from a plain program's by a relative error of at most 0.03.
Values may be sent and summed in bfloat16 or wider, within the bound.
A program may use at most 64 MiB of HBM per device.

v0:
```python
import jax
import jax.numpy as jnp
from jax import lax
from jax.sharding import PartitionSpec as P

HD = 128
HEADS = 32
KVH = 4
TICKS = 3


adapter_scale = 2.0


def passed_along(value, axis, steps):
    count = lax.axis_size(axis)
    pairs = [(source, (source + steps) % count) for source in range(count)]
    return lax.ppermute(value, axis, pairs)


def widen_rows(share_rows):
    return lax.all_gather(share_rows, "tp", axis=1, tiled=True)


def attend(query_rows, cache, request_lengths):
    owned = query_rows.shape[0]
    group = HEADS // KVH
    context = cache.shape[1]
    qh = query_rows.reshape(owned, KVH, group, HD)
    keys = cache[:, :, : KVH * HD].reshape(owned, context, KVH, HD)
    values = cache[:, :, KVH * HD :].reshape(owned, context, KVH, HD)
    scores = jnp.einsum("rkgh,rckh->rkgc", qh, keys, preferred_element_type=jnp.float32) * HD ** (
        -0.5
    )
    valid = (jnp.arange(context, dtype=jnp.int32)[None, :] < request_lengths[:, None])[
        :, None, None, :
    ]
    scores = jnp.where(valid, scores, -1e30)
    top = jnp.max(scores, axis=-1, keepdims=True)
    expo = jnp.where(valid, jnp.exp(scores - top), 0.0)
    weights = (expo / jnp.sum(expo, axis=-1, keepdims=True)).astype(jnp.bfloat16)
    attn = jnp.einsum("rkgc,rckh->rkgh", weights, values, preferred_element_type=jnp.float32)
    return attn.reshape(owned, KVH * group * HD).astype(jnp.bfloat16)


def local(
    hidden_entering,
    layer_norm_gain,
    query_matrix,
    output_matrix,
    adapter_down_weight,
    adapter_up_weight,
    key_value_cache,
    adapter_index,
    cached_lengths,
):
    sections = lax.axis_size("section")
    parts = lax.axis_size("tp")
    section = lax.axis_index("section")
    member = lax.axis_index("tp")
    request_rows = hidden_entering.shape[1]
    width = layer_norm_gain.shape[1]
    share = width // parts
    owned = request_rows // parts
    gain = layer_norm_gain[0].astype(jnp.float32)
    w_query = query_matrix[0]
    w_output = output_matrix[0]
    down_matrix = adapter_down_weight[0]
    up_matrix = adapter_up_weight[0]
    adapters = down_matrix.shape[0]
    rank_share = down_matrix.shape[1]
    rank_full = up_matrix.shape[1]
    down_flat = down_matrix.reshape(adapters * rank_share, width)
    flat_up_matrix = up_matrix.reshape(adapters * rank_full, up_matrix.shape[2])
    collected = []
    hidden_full = widen_rows(hidden_entering[0])
    for step_index in range(TICKS):
        group_index = (section - step_index) % sections
        request_adapters = lax.dynamic_index_in_dim(adapter_index, group_index, 0, keepdims=False)
        lens_all = lax.dynamic_index_in_dim(cached_lengths, group_index, 0, keepdims=False)
        request_lengths = lax.dynamic_slice_in_dim(lens_all, member * owned, owned)
        xf = hidden_full.astype(jnp.float32)
        inv = lax.rsqrt(jnp.mean(xf * xf, axis=-1, keepdims=True) + 1e-05)
        normed = (xf * inv * gain[None, :]).astype(jnp.bfloat16)
        base_query = jnp.dot(normed, w_query, preferred_element_type=jnp.float32)
        onehot = (
            request_adapters[:, None] == jnp.arange(adapters, dtype=jnp.int32)[None, :]
        ).astype(jnp.float32)
        u_all = lax.dot_general(
            normed, down_flat, (((1,), (1,)), ((), ())), preferred_element_type=jnp.float32
        )
        u_all = u_all.reshape(request_rows, adapters, rank_share)
        u_part = jnp.sum(u_all * onehot[:, :, None], axis=1).astype(jnp.bfloat16)
        u_whole = lax.all_gather(u_part, "tp", axis=1, tiled=True)
        spread_rows = (onehot.astype(jnp.bfloat16)[:, :, None] * u_whole[:, None, :]).reshape(
            request_rows, adapters * rank_full
        )
        adapter_delta = jnp.dot(spread_rows, flat_up_matrix, preferred_element_type=jnp.float32)
        query_slice = (base_query + adapter_scale * adapter_delta).astype(jnp.bfloat16)
        query_owned = lax.all_to_all(query_slice, "tp", split_axis=0, concat_axis=1, tiled=True)
        attn_owned = attend(query_owned, key_value_cache[0, step_index], request_lengths)
        attn_part = lax.all_to_all(attn_owned, "tp", split_axis=1, concat_axis=0, tiled=True)
        partial_value = jnp.dot(attn_part, w_output, preferred_element_type=jnp.float32)
        total = lax.psum(partial_value.astype(jnp.bfloat16), "tp").astype(jnp.float32)
        x_next = (hidden_full.astype(jnp.float32) + total).astype(jnp.bfloat16)
        collected.append(lax.dynamic_slice_in_dim(x_next, member * share, share, 1))
        if step_index + 1 < TICKS:
            hidden_full = passed_along(x_next, "section", 1)
    return jnp.stack(collected, axis=0)[None]


def solution(mesh):
    placed = (
        P("section", None, "tp"),
        P("section", None),
        P("section", None, "tp"),
        P("section", "tp", None),
        P("section", None, "tp", None),
        P("section", None, None, "tp"),
        P("section", None, "tp", None, None),
        P(),
        P(),
    )
    return jax.shard_map(
        local, mesh=mesh, in_specs=placed, out_specs=P("section", None, None, "tp"), check_vma=False
    )
```

profile of v0, /device:TPU:0, one launch (start us, length us, event | category | flops | bytes accessed | tf_op | source)
XLA Modules:
  0.0 311.8 jit_solution(11390344349135380308)
XLA Ops:
  6.5 0.8 fusion.81
  7.4 0.1 copy.31
  7.5 0.8 mul.220
  8.3 11.0 %all-gather = bf16[1,16,8192]{2,1,0:T(8,128)(2,1)S(1)} all-gather(bf16[1,16,1024]{2,1,0:T(8,128)(2,1)} %param.9), channel_id=2, replica_groups=mesh['section'=4,'tp'=8] {'tp'}, dimensions={2}, use_global_device_ids=true | all-gather | bytes 294912 | tf_op jit(solution)/shard_map/all_gather | solution.py:22
  19.3 0.2 fusion.45
  19.5 0.4 fusion.38
  19.8 8.7 %all_gather.13 = bf16[16,64]{0,1:T(8,128)(2,1)S(1)} all-gather(bf16[16,8]{0,1:T(8,128)(2,1)S(1)} %fusion.38), channel_id=1, replica_groups=mesh['section'=4,'tp'=8] {'tp'}, dimensions={1}, use_global_device_ids=true | all-gather | bytes 2304 | tf_op jit(solution)/shard_map/all_gather | solution.py:94
  28.6 0.1 broadcast_multiply_fusion.2
  28.7 0.1 mul.192
  28.8 4.6 %fusion.10 = f32[16,512]{1,0:T(8,128)S(1)} fusion(bf16[1,8192,512]{2,1,0:T(8,128)(2,1)} %param.11, bf16[1,16,8192]{2,1,0:T(8,128)(2,1)S(1)} %all-gather, f32[8192]{0:T(1024)S(1)} %bitcast.139, f32[16]{0:T(128)S(1)} %add_rsqrt_fusion.2), kind=kOutput, calls=%fused_computation.13 | convolution fusion | flops 134742016 | bytes 8716352 | tf_op jit(solution)/shard_map/dot_general | solution.py:85
  33.4 0.1 fusion.37
  33.5 0.6 all_to_all.72
  34.2 3.3 %all-to-all-start = ((bf16[8,2,512]{2,1,0:T(2,128)(2,1)}), bf16[8,2,512]{2,1,0:T(2,128)(2,1)S(1)}, u32[]{:S(2)}, u32[]{:S(2)}) async-start(bf16[8,2,512]{2,1,0:T(2,128)(2,1)} %all_to_all.72), calls=%async_computation | async-start | bytes 32768 | tf_op jit(solution)/shard_map/all_to_all | solution.py:100
  37.8 4.4 %all-to-all-done = bf16[8,2,512]{2,1,0:T(2,128)(2,1)S(1)} async-done(((bf16[8,2,512]{2,1,0:T(2,128)(2,1)}), bf16[8,2,512]{2,1,0:T(2,128)(2,1)S(1)}, u32[]{:S(2)}, u32[]{:S(2)}) %all-to-all-start) | async-done | bytes 16416 | tf_op jit(solution)/shard_map/all_to_all | solution.py:100
  42.2 0.1 fusion.23
  42.4 0.2 fusion.85
  42.6 0.3 convolution_convert_fusion.5
  42.9 7.1 %all_to_all.96 = bf16[2,8,512]{2,0,1:T(2,128)(2,1)S(1)} all-to-all(bf16[2,8,512]{2,0,1:T(2,128)(2,1)S(1)} %copy.36), channel_id=1, replica_groups=mesh['section'=4,'tp'=8] {'tp'}, dimensions={1} | all-to-all | bytes 32768 | tf_op jit(solution)/shard_map/all_to_all | solution.py:102
  50.0 5.3 %convolution_convert_fusion.2 = bf16[16,8192]{1,0:T(8,128)(2,1)} fusion(bf16[16,512]{1,0:T(8,128)(2,1)S(1)} %all_to_all.77, bf16[1,512,8192]{2,1,0:T(8,128)(2,1)} %param.12), kind=kOutput, calls=%fused_computation.5 | convolution fusion | flops 134348800 | bytes 8667136 | tf_op jit(solution)/shard_map/dot_general | solution.py:103
  55.3 53.4 %all-reduce.4.cloned.1.call-done = bf16[16,8192]{1,0:T(8,128)(2,1)} async-done(((bf16[16,8192]{1,0:T(8,128)(2,1)}), bf16[16,8192]{1,0:T(8,128)(2,1)}) %all-reduce.4.cloned.1.call-update) | async-done | bytes 262160 | tf_op jit(solution)/shard_map/psum | solution.py:104
  108.7 1.0 fusion.48
  109.8 1.5 collective-permute-start
  111.3 0.1 copy.37
  111.4 7.4 %collective-permute-done = bf16[16,8192]{1,0:T(8,128)(2,1)S(1)} collective-permute-done((bf16[16,8192]{1,0:T(8,128)(2,1)S(1)}, bf16[16,8192]{1,0:T(8,128)(2,1)S(1)}, u32[]{:S(2)}, u32[]{:S(2)}) %collective-permute-start) | collective-permute-done | bytes 262176 | tf_op jit(solution)/shard_map/ppermute | solution.py:18
  118.9 0.2 fusion.41
  119.0 0.4 fusion.39
  119.4 8.0 %all_gather.14 = bf16[16,64]{0,1:T(8,128)(2,1)S(1)} all-gather(bf16[16,8]{0,1:T(8,128)(2,1)S(1)} %fusion.39), channel_id=1, replica_groups=mesh['section'=4,'tp'=8] {'tp'}, dimensions={1}, use_global_device_ids=true | all-gather | bytes 2304 | tf_op jit(solution)/shard_map/all_gather | solution.py:94
  127.5 0.1 broadcast_multiply_fusion.1
  127.6 0.1 mul.205
  127.7 0.1 convolution_multiply_fusion.3
  127.9 4.6 %fusion.34 = bf16[16,512]{1,0:T(8,128)(2,1)S(1)} fusion(f32[16,512]{1,0:T(8,128)S(1)} %convolution_multiply_fusion.3, bf16[1,8192,512]{2,1,0:T(8,128)(2,1)} %param.11, bf16[16,8192]{1,0:T(8,128)(2,1)S(1)} %collective-permute-done, f32[16]{0:T(128)S(1)} %add_rsqrt_fusion.1, f32[8192]{0:T(1024)S(1)} %bitcast.141), kind=kOutput, calls=%fused_computation.37 | convolution fusion | flops 134758400 | bytes 8732736 | tf_op jit(solution)/shard_map/dot_general | solution.py:85
  132.5 0.6 all_to_all.78
  133.1 3.3 %all-to-all-start.2 = ((bf16[8,2,512]{2,1,0:T(2,128)(2,1)}), bf16[8,2,512]{2,1,0:T(2,128)(2,1)S(1)}, u32[]{:S(2)}, u32[]{:S(2)}) async-start(bf16[8,2,512]{2,1,0:T(2,128)(2,1)} %all_to_all.78), calls=%async_computation.2 | async-start | bytes 32768 | tf_op jit(solution)/shard_map/all_to_all | solution.py:100
  136.6 4.6 %all-to-all-done.2 = bf16[8,2,512]{2,1,0:T(2,128)(2,1)S(1)} async-done(((bf16[8,2,512]{2,1,0:T(2,128)(2,1)}), bf16[8,2,512]{2,1,0:T(2,128)(2,1)S(1)}, u32[]{:S(2)}, u32[]{:S(2)}) %all-to-all-start.2) | async-done | bytes 16416 | tf_op jit(solution)/shard_map/all_to_all | solution.py:100
  141.2 0.1 fusion.22
  141.3 0.2 fusion.86
  141.5 0.3 convolution_convert_fusion.4
  141.8 7.1 %all_to_all.97 = bf16[2,8,512]{2,0,1:T(2,128)(2,1)S(1)} all-to-all(bf16[2,8,512]{2,0,1:T(2,128)(2,1)S(1)} %copy.42), channel_id=1, replica_groups=mesh['section'=4,'tp'=8] {'tp'}, dimensions={1} | all-to-all | bytes 32768 | tf_op jit(solution)/shard_map/all_to_all | solution.py:102
  149.0 5.3 %convolution_convert_fusion.1 = bf16[16,8192]{1,0:T(8,128)(2,1)} fusion(bf16[16,512]{1,0:T(8,128)(2,1)S(1)} %all_to_all.83, bf16[1,512,8192]{2,1,0:T(8,128)(2,1)} %param.12), kind=kOutput, calls=%fused_computation.4 | convolution fusion | flops 134348800 | bytes 8667136 | tf_op jit(solution)/shard_map/dot_general | solution.py:103
  154.3 51.3 %all-reduce.6.cloned.1.call-done = bf16[16,8192]{1,0:T(8,128)(2,1)} async-done(((bf16[16,8192]{1,0:T(8,128)(2,1)}), bf16[16,8192]{1,0:T(8,128)(2,1)}) %all-reduce.6.cloned.1.call-update) | async-done | bytes 262160 | tf_op jit(solution)/shard_map/psum | solution.py:104
  205.6 1.0 fusion.44
  206.6 1.5 collective-permute-start.1
  208.1 0.1 copy.43
  208.2 7.5 %collective-permute-done.1 = bf16[16,8192]{1,0:T(8,128)(2,1)S(1)} collective-permute-done((bf16[16,8192]{1,0:T(8,128)(2,1)S(1)}, bf16[16,8192]{1,0:T(8,128)(2,1)S(1)}, u32[]{:S(2)}, u32[]{:S(2)}) %collective-permute-start.1) | collective-permute-done | bytes 262176 | tf_op jit(solution)/shard_map/ppermute | solution.py:18
  215.7 0.2 multiply_reduce_fusion
  215.9 0.4 fusion.40
  216.2 8.0 %all_gather.15 = bf16[16,64]{0,1:T(8,128)(2,1)S(1)} all-gather(bf16[16,8]{0,1:T(8,128)(2,1)S(1)} %fusion.40), channel_id=1, replica_groups=mesh['section'=4,'tp'=8] {'tp'}, dimensions={1}, use_global_device_ids=true | all-gather | bytes 2304 | tf_op jit(solution)/shard_map/all_gather | solution.py:94
  224.3 0.1 broadcast_multiply_fusion
  224.4 0.1 mul.217
  224.5 0.1 convolution_multiply_fusion.1
  224.7 4.6 %fusion.31 = bf16[16,512]{1,0:T(8,128)(2,1)S(1)} fusion(f32[16,512]{1,0:T(8,128)S(1)} %convolution_multiply_fusion.1, bf16[1,8192,512]{2,1,0:T(8,128)(2,1)} %param.11, f32[16]{0:T(128)S(1)} %add_rsqrt_fusion, bf16[16,8192]{1,0:T(8,128)(2,1)S(1)} %collective-permute-done.1, f32[8192]{0:T(1024)S(1)} %bitcast.143), kind=kOutput, calls=%fused_computation.36 | convolution fusion | flops 134758400 | bytes 8732736 | tf_op jit(solution)/shard_map/dot_general | solution.py:85
  229.3 0.6 all_to_all.84
  229.9 3.3 %all-to-all-start.4 = ((bf16[8,2,512]{2,1,0:T(2,128)(2,1)}), bf16[8,2,512]{2,1,0:T(2,128)(2,1)S(1)}, u32[]{:S(2)}, u32[]{:S(2)}) async-start(bf16[8,2,512]{2,1,0:T(2,128)(2,1)} %all_to_all.84), calls=%async_computation.4 | async-start | bytes 32768 | tf_op jit(solution)/shard_map/all_to_all | solution.py:100
  233.3 4.7 %all-to-all-done.4 = bf16[8,2,512]{2,1,0:T(2,128)(2,1)S(1)} async-done(((bf16[8,2,512]{2,1,0:T(2,128)(2,1)}), bf16[8,2,512]{2,1,0:T(2,128)(2,1)S(1)}, u32[]{:S(2)}, u32[]{:S(2)}) %all-to-all-start.4) | async-done | bytes 16416 | tf_op jit(solution)/shard_map/all_to_all | solution.py:100
  238.0 0.1 fusion.21
  238.1 0.2 fusion.87
  238.3 0.3 convolution_convert_fusion.3
  238.6 0.6 copy.48
  239.2 3.3 %all-to-all-start.5 = ((bf16[2,8,512]{2,0,1:T(2,128)(2,1)}), bf16[2,8,512]{2,0,1:T(2,128)(2,1)S(1)}, u32[]{:S(2)}, u32[]{:S(2)}) async-start(bf16[2,8,512]{2,0,1:T(2,128)(2,1)} %copy.48), calls=%async_computation.5 | async-start | bytes 32768 | tf_op jit(solution)/shard_map/all_to_all | solution.py:102
  242.6 4.6 %all-to-all-done.5 = bf16[2,8,512]{2,0,1:T(2,128)(2,1)S(1)} async-done(((bf16[2,8,512]{2,0,1:T(2,128)(2,1)}), bf16[2,8,512]{2,0,1:T(2,128)(2,1)S(1)}, u32[]{:S(2)}, u32[]{:S(2)}) %all-to-all-start.5) | async-done | bytes 16416 | tf_op jit(solution)/shard_map/all_to_all | solution.py:102
  247.3 5.3 %convolution_convert_fusion = bf16[16,8192]{1,0:T(8,128)(2,1)} fusion(bf16[16,512]{1,0:T(8,128)(2,1)S(1)} %all_to_all.89, bf16[1,512,8192]{2,1,0:T(8,128)(2,1)} %param.12), kind=kOutput, calls=%fused_computation.3 | convolution fusion | flops 134348800 | bytes 8667136 | tf_op jit(solution)/shard_map/dot_general | solution.py:103
  252.7 51.2 %all-reduce.8.cloned.1.call-done = bf16[16,8192]{1,0:T(8,128)(2,1)} async-done(((bf16[16,8192]{1,0:T(8,128)(2,1)}), bf16[16,8192]{1,0:T(8,128)(2,1)}) %all-reduce.8.cloned.1.call-update) | async-done | bytes 262160 | tf_op jit(solution)/shard_map/psum | solution.py:104
  303.9 0.8 fusion.72
  304.6 0.7 maximum_bitcast_fusion
  (47 shorter events, 1.0 us)
Async XLA Ops:
  6.5 12.9 %copy-start = (bf16[1,4,8,8192]{3,2,1,0:T(8,128)(2,1)S(1)}, bf16[1,4,8,8192]{3,2,1,0:T(8,128)(2,1)}, u32[]{:S(2)}) copy-start(bf16[1,4,8,8192]{3,2,1,0:T(8,128)(2,1)} %param.13) | copy-start | bytes 1572868
  6.5 26.9 %copy-start.1 = (bf16[1,4,64,512]{3,2,1,0:T(8,128)(2,1)S(1)}, bf16[1,4,64,512]{3,2,1,0:T(8,128)(2,1)}, u32[]{:S(2)}) copy-start(bf16[1,4,64,512]{3,2,1,0:T(8,128)(2,1)} %param.14) | copy-start | bytes 786436
  6.5 31.1 %copy-start.2 = (bf16[1,3,2,32,1024]{4,3,2,1,0:T(8,128)(2,1)S(1)}, bf16[1,3,2,32,1024]{4,3,2,1,0:T(8,128)(2,1)}, u32[]{:S(2)}) copy-start(bf16[1,3,2,32,1024]{4,3,2,1,0:T(8,128)(2,1)} %param.15) | copy-start | bytes 1179652
  6.5 31.1 %copy-start.3 = (s32[4,16]{1,0:T(4,128)S(1)}, s32[4,16]{1,0:T(4,128)}, u32[]{:S(2)}) copy-start(s32[4,16]{1,0:T(4,128)} %param.17) | copy-start | bytes 772
  34.2 8.0 %all-to-all-start = ((bf16[8,2,512]{2,1,0:T(2,128)(2,1)}), bf16[8,2,512]{2,1,0:T(2,128)(2,1)S(1)}, u32[]{:S(2)}, u32[]{:S(2)}) async-start(bf16[8,2,512]{2,1,0:T(2,128)(2,1)} %all_to_all.72), calls=%async_computation | async-start | bytes 32768 | tf_op jit(solution)/shard_map/all_to_all | solution.py:100
  37.5 71.2 %all-reduce.4.cloned.1.call-start = ((), (), s32[]{:S(2)}) async-start(), calls=%async_computation.6 | async-start | bytes 524288 | tf_op jit(solution)/shard_map/psum | solution.py:104
  109.8 9.1 %collective-permute-start = (bf16[16,8192]{1,0:T(8,128)(2,1)S(1)}, bf16[16,8192]{1,0:T(8,128)(2,1)S(1)}, u32[]{:S(2)}, u32[]{:S(2)}) collective-permute-start(bf16[16,8192]{1,0:T(8,128)(2,1)S(1)} %fusion.48), channel_id=1, source_target_pairs={{0,8},{8,16},{16,24},{24,0},{1,9},{9,17},{17,25},{25,1},{2,10},{10... | collective-permute-start | bytes 786440 | tf_op jit(solution)/shard_map/ppermute | solution.py:18
  133.1 8.0 %all-to-all-start.2 = ((bf16[8,2,512]{2,1,0:T(2,128)(2,1)}), bf16[8,2,512]{2,1,0:T(2,128)(2,1)S(1)}, u32[]{:S(2)}, u32[]{:S(2)}) async-start(bf16[8,2,512]{2,1,0:T(2,128)(2,1)} %all_to_all.78), calls=%async_computation.2 | async-start | bytes 32768 | tf_op jit(solution)/shard_map/all_to_all | solution.py:100
  136.5 69.1 %all-reduce.6.cloned.1.call-start = ((), (), s32[]{:S(2)}) async-start(), calls=%async_computation.7 | async-start | bytes 524288 | tf_op jit(solution)/shard_map/psum | solution.py:104
  206.6 9.1 %collective-permute-start.1 = (bf16[16,8192]{1,0:T(8,128)(2,1)S(1)}, bf16[16,8192]{1,0:T(8,128)(2,1)S(1)}, u32[]{:S(2)}, u32[]{:S(2)}) collective-permute-start(bf16[16,8192]{1,0:T(8,128)(2,1)S(1)} %fusion.44), channel_id=1, source_target_pairs={{0,8},{8,16},{16,24},{24,0},{1,9},{9,17},{17,25},{25,1},{2,10},{10... | collective-permute-start | bytes 786440 | tf_op jit(solution)/shard_map/ppermute | solution.py:18
  229.9 8.0 %all-to-all-start.4 = ((bf16[8,2,512]{2,1,0:T(2,128)(2,1)}), bf16[8,2,512]{2,1,0:T(2,128)(2,1)S(1)}, u32[]{:S(2)}, u32[]{:S(2)}) async-start(bf16[8,2,512]{2,1,0:T(2,128)(2,1)} %all_to_all.84), calls=%async_computation.4 | async-start | bytes 32768 | tf_op jit(solution)/shard_map/all_to_all | solution.py:100
  239.2 8.0 %all-to-all-start.5 = ((bf16[2,8,512]{2,0,1:T(2,128)(2,1)}), bf16[2,8,512]{2,0,1:T(2,128)(2,1)S(1)}, u32[]{:S(2)}, u32[]{:S(2)}) async-start(bf16[2,8,512]{2,0,1:T(2,128)(2,1)} %copy.48), calls=%async_computation.5 | async-start | bytes 32768 | tf_op jit(solution)/shard_map/all_to_all | solution.py:102
  242.6 61.3 %all-reduce.8.cloned.1.call-start = ((), (), s32[]{:S(2)}) async-start(), calls=%async_computation.8 | async-start | bytes 524288 | tf_op jit(solution)/shard_map/psum | solution.py:104
Sparse Core Ops, SparseCore 0:
  55.5 53.2 all-reduce.3
  154.4 51.1 all-reduce.5
  252.7 51.1 all-reduce.7
where the time goes:
time: 313 us; the launch traced here: 312 us
  waiting for transfers between devices  189 us (60%)
  blocking collectives  50 us (16%)
  matrix products  32.4 us (10%)
  starting transfers between devices  16.5 us (5%)
  between operations  13.4 us (4%)
  other arithmetic  5.89 us (2%)
  local copies, waits for them, and re-layouts  4.52 us (1%)
    psum x3, waiting for transfers between devices, local(): lax.psum(partial_value.astype(jnp.bfloat16), 'tp').astype(jnp.float32)  156 us
    all_gather x3, blocking collectives, local(): u_whole = lax.all_gather(u_part, 'tp', axis=1, tiled=True)  24.8 us
    dot_general x3, matrix products, local(): jnp.dot(attn_part, w_output, preferred_element_type=jnp.float32)  15.9 us
    ppermute x2, waiting for transfers between devices, passed_along(): return lax.ppermute(value, axis, pairs)  14.9 us
    all_to_all x2, blocking collectives, local(): lax.all_to_all(attn_owned, 'tp', split_axis=1, concat_axis=0, tiled=True)  14.2 us
    dot_general x3, matrix products, local(): base_query = jnp.dot(normed, w_query, preferred_element_type=jnp.float32)  13.9 us
    all_to_all x3, waiting for transfers between devices, local(): lax.all_to_all(query_slice, 'tp', split_axis=0, concat_axis=1, tiled=True)  13.6 us
    all_gather x1, blocking collectives, widen_rows(): return lax.all_gather(share_rows, 'tp', axis=1, tiled=True)  11 us
  transfers between devices with their start and end apart: 9, of which 9 were waited for; matrix products, arithmetic and copies ran while one was open for 0% of the time, Pallas kernels for 0%

commit v1 on v0

v1 whole, which is shorter than its diff:
```python
import functools

import jax
import jax.numpy as jnp
from jax import lax
from jax.experimental import pallas as pl
from jax.experimental.pallas import tpu as pltpu
from jax.sharding import PartitionSpec as P

HD = 128
HEADS = 32
KVH = 4
ADAPTER_SCALE = 2.0
MESH = pl.DeviceIdType.MESH
BF16 = jnp.bfloat16
F32 = jnp.float32


def flipped(me, d):
    value, bit = me, 1
    while bit <= d:
        if d & bit:
            value = value + bit * (1 - 2 * ((me // bit) % 2))
        bit *= 2
    return value


def kernel(
    sections,
    parts,
    adapter_ref,
    lens_ref,
    x_ref,
    gain_ref,
    wq_hbm,
    wo_hbm,
    down_ref,
    up_ref,
    kv_hbm,
    out_ref,
    wq,
    wo,
    down32,
    kbuf,
    vbuf,
    xbuf,
    hbuf,
    ubuf,
    rbuf,
    sbuf,
    load_sem,
    kv_send,
    kv_recv,
    x_send,
    x_recv,
    u_send,
    u_recv,
    r_send,
    r_recv,
    z_send,
    z_recv,
):
    section = lax.axis_index("section")
    me = lax.axis_index("tp")
    ticks = kbuf.shape[0]
    rows, share = x_ref.shape[1], x_ref.shape[2]
    width = parts * share
    owned = kv_hbm.shape[2]
    context = kv_hbm.shape[3]
    feats = wq.shape[1]
    heads = feats // HD
    group = HEADS // KVH
    adapters, rank_share = down_ref.shape[1], down_ref.shape[2]
    rank_full = up_ref.shape[2]
    ranks = adapters * rank_share
    nxt = (section + 1) % sections
    prv = (section + sections - 1) % sections

    wq_copies = []
    for d in range(parts):
        lo = pl.multiple_of(flipped(me, d) * share, share)
        wq_copies.append(
            pltpu.make_async_copy(
                wq_hbm.at[0, pl.ds(lo, share), :], wq.at[pl.ds(lo, share), :], load_sem.at[d]
            )
        )
    wo_copy = pltpu.make_async_copy(wo_hbm.at[0], wo, load_sem.at[parts])
    for copy in wq_copies:
        copy.start()
    wo_copy.start()

    barrier = pltpu.get_barrier_semaphore()
    for d in range(1, parts):
        pl.semaphore_signal(
            barrier, inc=1, device_id=(section, flipped(me, d)), device_id_type=MESH
        )
    pl.semaphore_signal(barrier, inc=1, device_id=(nxt, me), device_id_type=MESH)
    pl.semaphore_signal(barrier, inc=1, device_id=(prv, me), device_id_type=MESH)
    for a in range(adapters):
        down32[a * rank_share : (a + 1) * rank_share, :] = down_ref[0, a].astype(F32)
    xbuf[0, 0] = x_ref[0]
    pl.semaphore_wait(barrier, parts + 1)

    def send(src, dst, ssem, rsem, device):
        copy = pltpu.make_async_remote_copy(
            src_ref=src,
            dst_ref=dst,
            send_sem=ssem,
            recv_sem=rsem,
            device_id=device,
            device_id_type=MESH,
        )
        copy.start()
        return copy

    far_first = list(range(parts - 1, 0, -1))
    pending = []

    def spread_x(t, src):
        copies = [None] * parts
        for d in far_first:
            copies[d] = send(
                src, xbuf.at[t, d], x_send.at[t, d], x_recv.at[t, d], (section, flipped(me, d))
            )
        pending.extend(c for c in copies if c is not None)
        return copies

    x_copies = spread_x(0, x_ref.at[0])

    def kv_head(device):
        return (device * heads) // group

    mine = pl.ds(pl.multiple_of(me * owned, owned), owned)
    kv_copies = []
    for d in [0] + far_first:
        peer = flipped(me, d)
        kcol = pl.multiple_of(kv_head(peer) * HD, HD)
        vcol = pl.multiple_of(KVH * HD + kv_head(peer) * HD, HD)
        for i, (col, buf) in enumerate(((kcol, kbuf), (vcol, vbuf))):
            src = kv_hbm.at[0, :, :, :, pl.ds(col, HD)]
            dst = buf.at[:, mine]
            if d == 0:
                copy = pltpu.make_async_copy(src, dst, kv_recv.at[i, 0])
                copy.start()
            else:
                copy = send(src, dst, kv_send.at[i, d], kv_recv.at[i, d], (section, peer))
                pending.append(copy)
            kv_copies.append((d, copy))

    row = lax.broadcasted_iota(jnp.int32, (ranks, adapters * rank_full), 0)
    col = lax.broadcasted_iota(jnp.int32, (ranks, adapters * rank_full), 1)
    place = jnp.where(
        col == (row // rank_share) * rank_full + me * rank_share + row % rank_share, 1.0, 0.0
    ).astype(BF16)

    for t in range(ticks):
        gidx = (section + sections - t) % sections
        r_id = lax.broadcasted_iota(jnp.int32, (rows, ranks), 0)
        a_id = lax.broadcasted_iota(jnp.int32, (rows, ranks), 1) // rank_share
        chosen = jnp.zeros((rows, ranks), jnp.int32)
        c_id = lax.broadcasted_iota(jnp.int32, (1, rows * context), 1)
        lens = jnp.zeros((1, rows * context), jnp.int32)
        for r in range(rows):
            chosen = jnp.where(r_id == r, adapter_ref[gidx, r], chosen)
            lens = jnp.where(c_id // context == r, lens_ref[gidx, r], lens)
        onehot = jnp.where(chosen == a_id, 1.0, 0.0)
        m_row = lax.broadcasted_iota(jnp.int32, (heads * rows, rows * context), 0) % rows
        m_col = lax.broadcasted_iota(jnp.int32, (heads * rows, rows * context), 1)
        valid = (m_row == m_col // context) & (m_col % context < lens)

        if t > 0:
            z_copy.wait()
            x_copies = spread_x(t, xbuf.at[t, 0])

        squares = jnp.zeros((rows, 1), F32)
        acc_u = jnp.zeros((rows, ranks), F32)
        acc_q = jnp.zeros((rows, feats), F32)
        for d in range(parts):
            if d > 0:
                x_copies[d].wait_recv()
            lo = pl.multiple_of(flipped(me, d) * share, share)
            xf = xbuf[t, d].astype(F32)
            squares += jnp.sum(xf * xf, axis=-1, keepdims=True)
            h = (xf * gain_ref[:, pl.ds(lo, share)].astype(F32)).astype(BF16)
            hbuf[d] = h
            acc_u += lax.dot_general(
                h,
                down32[:, pl.ds(lo, share)].astype(BF16),
                (((1,), (1,)), ((), ())),
                preferred_element_type=F32,
            )
            if d < parts // 2:
                if t == 0:
                    wq_copies[d].wait()
                acc_q += jnp.dot(h, wq[pl.ds(lo, share), :], preferred_element_type=F32)
        inv = lax.rsqrt(squares * (1.0 / width) + 1e-05)
        u_own = (acc_u * inv * onehot).astype(BF16)
        u_placed = jnp.dot(u_own, place, preferred_element_type=F32)
        ubuf[t, 0] = u_placed.astype(BF16)
        u_copies = [None] * parts
        for d in far_first:
            u_copies[d] = send(
                ubuf.at[t, 0],
                ubuf.at[t, d],
                u_send.at[t, d],
                u_recv.at[t, d],
                (section, flipped(me, d)),
            )
            pending.append(u_copies[d])
        for d in range(parts // 2, parts):
            lo = pl.multiple_of(flipped(me, d) * share, share)
            if t == 0:
                wq_copies[d].wait()
            acc_q += jnp.dot(hbuf[d], wq[pl.ds(lo, share), :], preferred_element_type=F32)
        u_sum = u_placed
        for d in range(1, parts):
            u_copies[d].wait_recv()
            u_sum += ubuf[t, d].astype(F32)
        up = up_ref[0].reshape(adapters * rank_full, feats)
        delta = jnp.dot(u_sum.astype(BF16), up, preferred_element_type=F32)
        query = (acc_q * inv + ADAPTER_SCALE * delta).astype(BF16)

        if t == 0:
            for d, copy in kv_copies:
                if d == 0:
                    copy.wait()
                else:
                    copy.wait_recv()
        qh = jnp.concatenate([query[:, i * HD : (i + 1) * HD] for i in range(heads)], axis=0)
        keys = kbuf[t].reshape(rows * context, HD)
        values = vbuf[t].reshape(rows * context, HD)
        scores = lax.dot_general(
            qh, keys, (((1,), (1,)), ((), ())), preferred_element_type=F32
        ) * HD ** (-0.5)
        scores = jnp.where(valid, scores, -1e30)
        top = jnp.max(scores, axis=-1, keepdims=True)
        expo = jnp.where(valid, jnp.exp(scores - top), 0.0)
        weights = (expo / jnp.sum(expo, axis=-1, keepdims=True)).astype(BF16)
        attn = jnp.dot(weights, values, preferred_element_type=F32).astype(BF16)
        attn = jnp.concatenate([attn[i * rows : (i + 1) * rows] for i in range(heads)], axis=1)

        if t == 0:
            wo_copy.wait()
        r_copies = [None] * parts
        for d in far_first:
            peer = flipped(me, d)
            lo = pl.multiple_of(peer * share, share)
            sbuf[t, d] = jnp.dot(
                attn, wo[:, pl.ds(lo, share)], preferred_element_type=F32
            ).astype(BF16)
            r_copies[d] = send(
                sbuf.at[t, d], rbuf.at[t, d], r_send.at[t, d], r_recv.at[t, d], (section, peer)
            )
            pending.append(r_copies[d])
        lo = pl.multiple_of(me * share, share)
        total = (
            jnp.dot(attn, wo[:, pl.ds(lo, share)], preferred_element_type=F32)
            .astype(BF16)
            .astype(F32)
        )
        for d in range(1, parts):
            r_copies[d].wait_recv()
            total += rbuf[t, d].astype(F32)
        result = (xbuf[t, 0].astype(F32) + total).astype(BF16)
        out_ref[0, t] = result
        if t + 1 < ticks:
            z_copy = send(
                out_ref.at[0, t], xbuf.at[t + 1, 0], z_send.at[t], z_recv.at[t], (nxt, me)
            )

    for copy in pending:
        copy.wait_send()


def local(
    hidden_entering,
    layer_norm_gain,
    query_matrix,
    output_matrix,
    adapter_down_weight,
    adapter_up_weight,
    key_value_cache,
    adapter_index,
    cached_lengths,
):
    sections = lax.axis_size("section")
    parts = lax.axis_size("tp")
    rows, share = hidden_entering.shape[1:]
    ticks, _, context, _ = key_value_cache.shape[1:]
    width, feats = query_matrix.shape[1:]
    adapters, rank_share = adapter_down_weight.shape[1:3]
    rank_full = adapter_up_weight.shape[2]
    vmem = pl.BlockSpec(memory_space=pltpu.VMEM)
    smem = pl.BlockSpec(memory_space=pltpu.SMEM)
    hbm = pl.BlockSpec(memory_space=pl.ANY)
    dma = pltpu.SemaphoreType.DMA
    return pl.pallas_call(
        functools.partial(kernel, sections, parts),
        out_shape=jax.ShapeDtypeStruct((1, ticks, rows, share), BF16),
        in_specs=[smem, smem, vmem, vmem, hbm, hbm, vmem, vmem, hbm],
        out_specs=vmem,
        scratch_shapes=[
            pltpu.VMEM((width, feats), BF16),
            pltpu.VMEM((feats, width), BF16),
            pltpu.VMEM((adapters * rank_share, width), F32),
            pltpu.VMEM((ticks, rows, context, HD), BF16),
            pltpu.VMEM((ticks, rows, context, HD), BF16),
            pltpu.VMEM((ticks, parts, rows, share), BF16),
            pltpu.VMEM((parts, rows, share), BF16),
            pltpu.VMEM((ticks, parts, rows, adapters * rank_full), BF16),
            pltpu.VMEM((ticks, parts, rows, share), BF16),
            pltpu.VMEM((ticks, parts, rows, share), BF16),
            dma((parts + 1,)),
            dma((2, parts)),
            dma((2, parts)),
            dma((ticks, parts)),
            dma((ticks, parts)),
            dma((ticks, parts)),
            dma((ticks, parts)),
            dma((ticks, parts)),
            dma((ticks, parts)),
            dma((ticks,)),
            dma((ticks,)),
        ],
        compiler_params=pltpu.CompilerParams(
            collective_id=0, has_side_effects=True, vmem_limit_bytes=56 << 20
        ),
    )(
        adapter_index,
        cached_lengths,
        hidden_entering,
        layer_norm_gain,
        query_matrix,
        output_matrix,
        adapter_down_weight,
        adapter_up_weight,
        key_value_cache,
    )


def solution(mesh):
    placed = (
        P("section", None, "tp"),
        P("section", None),
        P("section", None, "tp"),
        P("section", "tp", None),
        P("section", None, "tp", None),
        P("section", None, None, "tp"),
        P("section", None, "tp", None, None),
        P(),
        P(),
    )
    return jax.shard_map(
        local, mesh=mesh, in_specs=placed, out_specs=P("section", None, None, "tp"), check_vma=False
    )
```

time: 313 us -> 64.8 us (0.21)
  waiting for transfers between devices: 189 us -> 0 us
  Pallas kernels: 0 us -> 63.1 us
  blocking collectives: 50 us -> 0 us
  matrix products: 32.4 us -> 0 us
  starting transfers between devices: 16.5 us -> 0 us
  between operations: 13.4 us -> 0.01 us
  other arithmetic: 5.89 us -> 0 us
    psum x3 -> x0, waiting for transfers between devices: 156 us -> none  [local(): lax.psum(partial_value.astype(jnp.bfloat16), 'tp').astype(jnp.float32)]
    pallas_call x0 -> x1, Pallas kernels: none -> 63.1 us  [local(): pl.pallas_call(functools.partial(kernel, sections, parts), out_shape=jax....]
    all_gather x4 -> x0, blocking collectives: 35.8 us -> none  [the longest x3 24.8 us: local(): u_whole = lax.all_gather(u_part, 'tp', axis=1, tiled=True)]
    dot_general x18 -> x0, matrix products: 32.4 us -> none  [the longest x3 15.9 us: local(): jnp.dot(attn_part, w_output, preferred_element_type=jnp.float32)]
    all_to_all x4 -> x0, waiting for transfers between devices: 18.2 us -> none  [the longest x3 13.6 us: local(): lax.all_to_all(query_slice, 'tp', split_axis=0, concat_axis=1, tiled=True)]
    ppermute x2 -> x0, waiting for transfers between devices: 14.9 us -> none  [passed_along(): return lax.ppermute(value, axis, pairs)]
    all_to_all x2 -> x0, blocking collectives: 14.2 us -> none  [local(): lax.all_to_all(attn_owned, 'tp', split_axis=1, concat_axis=0, tiled=True)]
    all_to_all x4 -> x0, starting transfers between devices: 13.3 us -> none  [the longest x3 10 us: local(): lax.all_to_all(query_slice, 'tp', split_axis=0, concat_axis=1, tiled=True)]
  transfers between devices with their start and end apart: 9 -> 0, of which waited for: 9 -> 0; matrix products, arithmetic and copies ran while one was open for 0% -> 0% of each run, Pallas kernels for 0% -> 0%
where the time goes in v1:
time: 64.8 us; the launch traced here: 64.6 us
  Pallas kernels  63.1 us (97%)
  local copies, waits for them, and re-layouts  1.54 us (2%)
    pallas_call x1, Pallas kernels, local(): pl.pallas_call(functools.partial(kernel, sections, parts), out_shape=jax....  63.1 us
    unnamed x1, local copies, waits for them, and re-layouts  1.54 us

profile of v1, /device:TPU:0, one launch (start us, length us, event | category | flops | bytes accessed | tf_op | source)
XLA Modules:
  0.0 64.6 jit_solution(8888533716982060164)
XLA Ops:
  0.0 63.1 %shard_map.91 = bf16[1,3,16,1024]{3,2,1,0:T(8,128)(2,1)} custom-call(s32[4,16]{1,0:T(4,128)} %adapter_ref.1, s32[4,16]{1,0:T(4,128)} %lens_ref.1, bf16[1,16,1024]{2,1,0:T(8,128)(2,1)} %x_ref.1, bf16[1,8192]{1,0:T(2,128)(2,1)} %gain_ref.1, bf16[1,8192,512]{2,1,0:T(8,128)(2,1)} %wq_hbm.1, bf16[1,512,8192]{2,1,0:T(8,128)(2,1)} %wo_hbm.1, ...), custom_call_target="tpu_custom_call" | custom-call | tf_op jit(solution)/shard_map/pallas_call | solution.py:297
  63.1 1.5 %copy.11 = bf16[1,3,16,1024]{3,2,1,0:T(8,128)(2,1)} copy(bf16[1,3,16,1024]{3,2,1,0:T(8,128)(2,1)} %shard_map.91) | data formatting | bytes 196608

commit v2 on v1

--- a/solution.py
+++ b/solution.py
@@ -41,6 +41,10 @@
     wq,
     wo,
     down32,
+    dparts,
+    dcols32,
+    dcols,
+    upbuf,
     kbuf,
     vbuf,
     xbuf,
@@ -49,6 +53,8 @@
     rbuf,
     sbuf,
     load_sem,
+    d_send,
+    d_recv,
     kv_send,
     kv_recv,
     x_send,
@@ -125,39 +131,109 @@
         pending.extend(c for c in copies if c is not None)
         return copies
 
+    def spread_u(t):
+        copies = [None] * parts
+        for d in far_first:
+            copies[d] = send(
+                ubuf.at[t, 0],
+                ubuf.at[t, d],
+                u_send.at[t, d],
+                u_recv.at[t, d],
+                (section, flipped(me, d)),
+            )
+            pending.append(copies[d])
+        return copies
+
     x_copies = spread_x(0, x_ref.at[0])
 
     def kv_head(device):
         return (device * heads) // group
 
-    mine = pl.ds(pl.multiple_of(me * owned, owned), owned)
-    kv_copies = []
-    for d in [0] + far_first:
-        peer = flipped(me, d)
-        kcol = pl.multiple_of(kv_head(peer) * HD, HD)
-        vcol = pl.multiple_of(KVH * HD + kv_head(peer) * HD, HD)
-        for i, (col, buf) in enumerate(((kcol, kbuf), (vcol, vbuf))):
-            src = kv_hbm.at[0, :, :, :, pl.ds(col, HD)]
-            dst = buf.at[:, mine]
-            if d == 0:
-                copy = pltpu.make_async_copy(src, dst, kv_recv.at[i, 0])
-                copy.start()
-            else:
-                copy = send(src, dst, kv_send.at[i, d], kv_recv.at[i, d], (section, peer))
+    def rows_of(device):
+        return pl.ds(pl.multiple_of(device * owned, owned), owned)
+
+    partner = flipped(me, 1)
+    kv_copies = {}
+
+    def send_cache(t):
+        for d in [0] + [e for e in far_first if e % 2 == 0] + [1]:
+            peer = flipped(me, d)
+            for i, buf in enumerate((kbuf, vbuf)):
+                col = pl.multiple_of(i * KVH * HD + kv_head(peer) * HD, HD)
+                src = kv_hbm.at[0, t, :, :, pl.ds(col, HD)]
+                dst = buf.at[t, rows_of(me)]
+                if d == 0:
+                    copy = pltpu.make_async_copy(src, dst, kv_recv.at[t, i, 0])
+                    copy.start()
+                else:
+                    copy = send(
+                        src, dst, kv_send.at[t, i, d], kv_recv.at[t, i, d], (section, peer)
+                    )
+                    pending.append(copy)
+                kv_copies[t, i, d] = copy
+
+    def forward_cache(t):
+        for d in range(2, parts, 2):
+            for i, buf in enumerate((kbuf, vbuf)):
+                kv_copies[t, i, d].wait_recv()
+                block = buf.at[t, rows_of(flipped(me, d))]
+                copy = send(
+                    block,
+                    block,
+                    kv_send.at[t, i, d + 1],
+                    kv_recv.at[t, i, d + 1],
+                    (section, partner),
+                )
                 pending.append(copy)
-            kv_copies.append((d, copy))
+                kv_copies[t, i, d + 1] = copy
+
+    def wait_cache(t):
+        for i in range(2):
+            kv_copies[t, i, 0].wait()
+            for d in range(1, parts):
+                if d == 1 or d % 2 == 1:
+                    kv_copies[t, i, d].wait_recv()
+
+    d_copies = {}
+
+    def send_down(peers):
+        for d in peers:
+            peer = flipped(me, d)
+            lo = pl.multiple_of(peer * share, share)
+            d_copies[d] = send(
+                down_ref.at[0, :, :, pl.ds(lo, share)],
+                dparts.at[me],
+                d_send.at[d],
+                d_recv.at[d],
+                (section, peer),
+            )
+            pending.append(d_copies[d])
+
+    down_first = [d for d in far_first if d >= parts - parts // 4 or d == 1]
+    down_later = [d for d in far_first if d not in down_first]
+    send_cache(0)
+    my_cols = pl.ds(pl.multiple_of(me * share, share), share)
+    dparts[me] = down_ref[0, :, :, my_cols]
+    send_down(down_first)
 
     row = lax.broadcasted_iota(jnp.int32, (ranks, adapters * rank_full), 0)
     col = lax.broadcasted_iota(jnp.int32, (ranks, adapters * rank_full), 1)
-    place = jnp.where(
-        col == (row // rank_share) * rank_full + me * rank_share + row % rank_share, 1.0, 0.0
-    ).astype(BF16)
+    place = jnp.where(col == me * ranks + row, 1.0, 0.0).astype(BF16)
+    full = adapters * rank_full
+    row = lax.broadcasted_iota(jnp.int32, (full, full), 0)
+    col = lax.broadcasted_iota(jnp.int32, (full, full), 1)
+    source = (
+        (row // rank_share) % adapters * rank_full + row // ranks * rank_share + row % rank_share
+    )
+    order = jnp.where(col == source, 1.0, 0.0).astype(BF16)
+    up = jnp.dot(order, up_ref[0].reshape(full, feats), preferred_element_type=F32).astype(BF16)
+    upbuf[...] = up
 
     for t in range(ticks):
         gidx = (section + sections - t) % sections
-        r_id = lax.broadcasted_iota(jnp.int32, (rows, ranks), 0)
-        a_id = lax.broadcasted_iota(jnp.int32, (rows, ranks), 1) // rank_share
-        chosen = jnp.zeros((rows, ranks), jnp.int32)
+        r_id = lax.broadcasted_iota(jnp.int32, (rows, full), 0)
+        a_id = lax.broadcasted_iota(jnp.int32, (rows, full), 1) // rank_share % adapters
+        chosen = jnp.zeros((rows, full), jnp.int32)
         c_id = lax.broadcasted_iota(jnp.int32, (1, rows * context), 1)
         lens = jnp.zeros((1, rows * context), jnp.int32)
         for r in range(rows):
@@ -169,8 +245,14 @@
         valid = (m_row == m_col // context) & (m_col % context < lens)
 
         if t > 0:
-            z_copy.wait()
+            z_copy.wait_recv()
             x_copies = spread_x(t, xbuf.at[t, 0])
+            h = (xbuf[t, 0].astype(F32) * gain_ref[:, my_cols].astype(F32)).astype(BF16)
+            u_part = lax.dot_general(
+                h, dcols[...], (((1,), (1,)), ((), ())), preferred_element_type=F32
+            )
+            ubuf[t, 0] = u_part.astype(BF16)
+            u_copies = spread_u(t)
 
         squares = jnp.zeros((rows, 1), F32)
         acc_u = jnp.zeros((rows, ranks), F32)
@@ -182,50 +264,42 @@
             xf = xbuf[t, d].astype(F32)
             squares += jnp.sum(xf * xf, axis=-1, keepdims=True)
             h = (xf * gain_ref[:, pl.ds(lo, share)].astype(F32)).astype(BF16)
-            hbuf[d] = h
-            acc_u += lax.dot_general(
-                h,
-                down32[:, pl.ds(lo, share)].astype(BF16),
-                (((1,), (1,)), ((), ())),
-                preferred_element_type=F32,
-            )
-            if d < parts // 2:
+            if t == 0:
+                hbuf[d] = h
+                acc_u += lax.dot_general(
+                    h,
+                    down32[:, pl.ds(lo, share)].astype(BF16),
+                    (((1,), (1,)), ((), ())),
+                    preferred_element_type=F32,
+                )
+            if t > 0 or d < parts // 2:
                 if t == 0:
                     wq_copies[d].wait()
                 acc_q += jnp.dot(h, wq[pl.ds(lo, share), :], preferred_element_type=F32)
         inv = lax.rsqrt(squares * (1.0 / width) + 1e-05)
-        u_own = (acc_u * inv * onehot).astype(BF16)
-        u_placed = jnp.dot(u_own, place, preferred_element_type=F32)
-        ubuf[t, 0] = u_placed.astype(BF16)
-        u_copies = [None] * parts
-        for d in far_first:
-            u_copies[d] = send(
-                ubuf.at[t, 0],
-                ubuf.at[t, d],
-                u_send.at[t, d],
-                u_recv.at[t, d],
-                (section, flipped(me, d)),
-            )
-            pending.append(u_copies[d])
-        for d in range(parts // 2, parts):
-            lo = pl.multiple_of(flipped(me, d) * share, share)
-            if t == 0:
+        if t == 0:
+            u_own = (acc_u * inv).astype(BF16)
+            u_sum = jnp.dot(u_own, place, preferred_element_type=F32)
+            ubuf[t, 0] = u_sum.astype(BF16)
+            u_copies = spread_u(t)
+            send_down(down_later)
+            for d in range(parts // 2, parts):
+                lo = pl.multiple_of(flipped(me, d) * share, share)
                 wq_copies[d].wait()
-            acc_q += jnp.dot(hbuf[d], wq[pl.ds(lo, share), :], preferred_element_type=F32)
-        u_sum = u_placed
+                acc_q += jnp.dot(hbuf[d], wq[pl.ds(lo, share), :], preferred_element_type=F32)
+        else:
+            u_sum = u_part
+        forward_cache(t)
         for d in range(1, parts):
             u_copies[d].wait_recv()
             u_sum += ubuf[t, d].astype(F32)
-        up = up_ref[0].reshape(adapters * rank_full, feats)
-        delta = jnp.dot(u_sum.astype(BF16), up, preferred_element_type=F32)
+        if t > 0:
+            u_sum = u_sum * inv
+        u_sum = (u_sum * onehot).astype(BF16)
+        delta = jnp.dot(u_sum, upbuf[...], preferred_element_type=F32)
         query = (acc_q * inv + ADAPTER_SCALE * delta).astype(BF16)
 
-        if t == 0:
-            for d, copy in kv_copies:
-                if d == 0:
-                    copy.wait()
-                else:
-                    copy.wait_recv()
+        wait_cache(t)
         qh = jnp.concatenate([query[:, i * HD : (i + 1) * HD] for i in range(heads)], axis=0)
         keys = kbuf[t].reshape(rows * context, HD)
         values = vbuf[t].reshape(rows * context, HD)
@@ -252,12 +326,21 @@
                 sbuf.at[t, d], rbuf.at[t, d], r_send.at[t, d], r_recv.at[t, d], (section, peer)
             )
             pending.append(r_copies[d])
-        lo = pl.multiple_of(me * share, share)
+        if t + 1 < ticks:
+            send_cache(t + 1)
         total = (
-            jnp.dot(attn, wo[:, pl.ds(lo, share)], preferred_element_type=F32)
+            jnp.dot(attn, wo[:, my_cols], preferred_element_type=F32)
             .astype(BF16)
             .astype(F32)
         )
+        if t == 0:
+            for d in range(1, parts):
+                d_copies[d].wait_recv()
+            for p in range(parts):
+                for a in range(adapters):
+                    lo = p * ranks + a * rank_share
+                    dcols32[lo : lo + rank_share, :] = dparts[p, a].astype(F32)
+            dcols[...] = dcols32[...].astype(BF16)
         for d in range(1, parts):
             r_copies[d].wait_recv()
             total += rbuf[t, d].astype(F32)
@@ -267,6 +350,7 @@
             z_copy = send(
                 out_ref.at[0, t], xbuf.at[t + 1, 0], z_send.at[t], z_recv.at[t], (nxt, me)
             )
+            pending.append(z_copy)
 
     for copy in pending:
         copy.wait_send()
@@ -303,6 +387,10 @@
             pltpu.VMEM((width, feats), BF16),
             pltpu.VMEM((feats, width), BF16),
             pltpu.VMEM((adapters * rank_share, width), F32),
+            pltpu.VMEM((parts, adapters, rank_share, share), BF16),
+            pltpu.VMEM((adapters * rank_full, share), F32),
+            pltpu.VMEM((adapters * rank_full, share), BF16),
+            pltpu.VMEM((adapters * rank_full, feats), BF16),
             pltpu.VMEM((ticks, rows, context, HD), BF16),
             pltpu.VMEM((ticks, rows, context, HD), BF16),
             pltpu.VMEM((ticks, parts, rows, share), BF16),
@@ -311,8 +399,10 @@
             pltpu.VMEM((ticks, parts, rows, share), BF16),
             pltpu.VMEM((ticks, parts, rows, share), BF16),
             dma((parts + 1,)),
-            dma((2, parts)),
-            dma((2, parts)),
+            dma((parts,)),
+            dma((parts,)),
+            dma((ticks, 2, parts)),
+            dma((ticks, 2, parts)),
             dma((ticks, parts)),
             dma((ticks, parts)),
             dma((ticks, parts)),

time: 64.8 us -> 60.7 us (0.937)
  Pallas kernels: 63.1 us -> 59 us
    pallas_call x1, Pallas kernels: 63.1 us -> 59 us  [local(): pl.pallas_call(functools.partial(kernel, sections, parts), out_shape=jax....]
where the time goes in v2:
time: 60.7 us; the launch traced here: 60.6 us
  Pallas kernels  59 us (97%)
  local copies, waits for them, and re-layouts  1.54 us (3%)
    pallas_call x1, Pallas kernels, local(): pl.pallas_call(functools.partial(kernel, sections, parts), out_shape=jax....  59 us
    unnamed x1, local copies, waits for them, and re-layouts  1.54 us

profile of v2, /device:TPU:0, one launch (start us, length us, event | category | flops | bytes accessed | tf_op | source)
XLA Modules:
  0.0 60.6 jit_solution(15832462419451609141)
XLA Ops:
  0.0 59.0 %shard_map.91 = bf16[1,3,16,1024]{3,2,1,0:T(8,128)(2,1)} custom-call(s32[4,16]{1,0:T(4,128)} %adapter_ref.1, s32[4,16]{1,0:T(4,128)} %lens_ref.1, bf16[1,16,1024]{2,1,0:T(8,128)(2,1)} %x_ref.1, bf16[1,8192]{1,0:T(2,128)(2,1)} %gain_ref.1, bf16[1,8192,512]{2,1,0:T(8,128)(2,1)} %wq_hbm.1, bf16[1,512,8192]{2,1,0:T(8,128)(2,1)} %wo_hbm.1, ...), custom_call_target="tpu_custom_call" | custom-call | tf_op jit(solution)/shard_map/pallas_call | solution.py:381
  59.0 1.5 %copy.11 = bf16[1,3,16,1024]{3,2,1,0:T(8,128)(2,1)} copy(bf16[1,3,16,1024]{3,2,1,0:T(8,128)(2,1)} %shard_map.91) | data formatting | bytes 196608

commit v3 on v2

--- a/solution.py
+++ b/solution.py
@@ -120,11 +120,18 @@
         return copy
 
     far_first = list(range(parts - 1, 0, -1))
+    relayed = [d for d in range(2, parts, 2) if d >= parts - parts // 4]
+    via_partner = [d + 1 for d in relayed]
+    direct = [d for d in far_first if d not in via_partner]
+    near = [d for d in range(2, parts) if d not in relayed and d not in via_partner]
+    near = [d for d in near if d % 2 == 0] + [d for d in near if d % 2 == 1]
+    arrival = [0, 1] + relayed + near + via_partner
+    partner = flipped(me, 1)
     pending = []
 
     def spread_x(t, src):
         copies = [None] * parts
-        for d in far_first:
+        for d in direct:
             copies[d] = send(
                 src, xbuf.at[t, d], x_send.at[t, d], x_recv.at[t, d], (section, flipped(me, d))
             )
@@ -152,7 +159,6 @@
     def rows_of(device):
         return pl.ds(pl.multiple_of(device * owned, owned), owned)
 
-    partner = flipped(me, 1)
     kv_copies = {}
 
     def send_cache(t):
@@ -257,9 +263,18 @@
         squares = jnp.zeros((rows, 1), F32)
         acc_u = jnp.zeros((rows, ranks), F32)
         acc_q = jnp.zeros((rows, feats), F32)
-        for d in range(parts):
+        for k, d in enumerate(arrival):
             if d > 0:
                 x_copies[d].wait_recv()
+            if d in relayed:
+                x_copies[d + 1] = send(
+                    xbuf.at[t, d],
+                    xbuf.at[t, d + 1],
+                    x_send.at[t, d + 1],
+                    x_recv.at[t, d + 1],
+                    (section, partner),
+                )
+                pending.append(x_copies[d + 1])
             lo = pl.multiple_of(flipped(me, d) * share, share)
             xf = xbuf[t, d].astype(F32)
             squares += jnp.sum(xf * xf, axis=-1, keepdims=True)
@@ -272,7 +287,7 @@
                     (((1,), (1,)), ((), ())),
                     preferred_element_type=F32,
                 )
-            if t > 0 or d < parts // 2:
+            if t > 0 or k < parts // 2:
                 if t == 0:
                     wq_copies[d].wait()
                 acc_q += jnp.dot(h, wq[pl.ds(lo, share), :], preferred_element_type=F32)
@@ -283,7 +298,7 @@
             ubuf[t, 0] = u_sum.astype(BF16)
             u_copies = spread_u(t)
             send_down(down_later)
-            for d in range(parts // 2, parts):
+            for d in arrival[parts // 2 :]:
                 lo = pl.multiple_of(flipped(me, d) * share, share)
                 wq_copies[d].wait()
                 acc_q += jnp.dot(hbuf[d], wq[pl.ds(lo, share), :], preferred_element_type=F32)
@@ -316,16 +331,34 @@
         if t == 0:
             wo_copy.wait()
         r_copies = [None] * parts
-        for d in far_first:
-            peer = flipped(me, d)
-            lo = pl.multiple_of(peer * share, share)
-            sbuf[t, d] = jnp.dot(
-                attn, wo[:, pl.ds(lo, share)], preferred_element_type=F32
-            ).astype(BF16)
-            r_copies[d] = send(
-                sbuf.at[t, d], rbuf.at[t, d], r_send.at[t, d], r_recv.at[t, d], (section, peer)
-            )
-            pending.append(r_copies[d])
+
+        def term(d):
+            lo = pl.multiple_of(flipped(me, d) * share, share)
+            return jnp.dot(attn, wo[:, pl.ds(lo, share)], preferred_element_type=F32).astype(BF16)
+
+        def send_term(d, slot, device):
+            r_copies[slot] = send(
+                sbuf.at[t, d],
+                rbuf.at[t, slot],
+                r_send.at[t, slot],
+                r_recv.at[t, slot],
+                (section, device),
+            )
+            pending.append(r_copies[slot])
+
+        for d in via_partner:
+            sbuf[t, d] = term(d)
+            send_term(d, d, partner)
+        for d in near:
+            sbuf[t, d] = term(d)
+            send_term(d, d, flipped(me, d))
+        for d in relayed:
+            pair = term(d).astype(F32)
+            r_copies[d + 1].wait_recv()
+            sbuf[t, d] = (pair + rbuf[t, d + 1].astype(F32)).astype(BF16)
+            send_term(d, d, flipped(me, d))
+        sbuf[t, 1] = term(1)
+        send_term(1, 1, partner)
         if t + 1 < ticks:
             send_cache(t + 1)
         total = (
@@ -341,7 +374,7 @@
                     lo = p * ranks + a * rank_share
                     dcols32[lo : lo + rank_share, :] = dparts[p, a].astype(F32)
             dcols[...] = dcols32[...].astype(BF16)
-        for d in range(1, parts):
+        for d in [1] + near + relayed:
             r_copies[d].wait_recv()
             total += rbuf[t, d].astype(F32)
         result = (xbuf[t, 0].astype(F32) + total).astype(BF16)

time: 60.7 us -> 59.3 us (0.977)
  Pallas kernels: 59 us -> 57.6 us
    pallas_call x1, Pallas kernels: 59 us -> 57.6 us  [local(): pl.pallas_call(functools.partial(kernel, sections, parts), out_shape=jax....]
where the time goes in v3:
time: 59.3 us; the launch traced here: 59.2 us
  Pallas kernels  57.6 us (97%)
  local copies, waits for them, and re-layouts  1.54 us (3%)
    pallas_call x1, Pallas kernels, local(): pl.pallas_call(functools.partial(kernel, sections, parts), out_shape=jax....  57.6 us
    unnamed x1, local copies, waits for them, and re-layouts  1.54 us

profile of v3, /device:TPU:0, one launch (start us, length us, event | category | flops | bytes accessed | tf_op | source)
XLA Modules:
  0.0 59.2 jit_solution(4360549248606376345)
XLA Ops:
  0.0 57.6 %shard_map.91 = bf16[1,3,16,1024]{3,2,1,0:T(8,128)(2,1)} custom-call(s32[4,16]{1,0:T(4,128)} %adapter_ref.1, s32[4,16]{1,0:T(4,128)} %lens_ref.1, bf16[1,16,1024]{2,1,0:T(8,128)(2,1)} %x_ref.1, bf16[1,8192]{1,0:T(2,128)(2,1)} %gain_ref.1, bf16[1,8192,512]{2,1,0:T(8,128)(2,1)} %wq_hbm.1, bf16[1,512,8192]{2,1,0:T(8,128)(2,1)} %wo_hbm.1, ...), custom_call_target="tpu_custom_call" | custom-call | tf_op jit(solution)/shard_map/pallas_call | solution.py:414
  57.6 1.5 %copy.11 = bf16[1,3,16,1024]{3,2,1,0:T(8,128)(2,1)} copy(bf16[1,3,16,1024]{3,2,1,0:T(8,128)(2,1)} %shard_map.91) | data formatting | bytes 196608

commit v4 on v3

--- a/solution.py
+++ b/solution.py
@@ -102,10 +102,16 @@
         )
     pl.semaphore_signal(barrier, inc=1, device_id=(nxt, me), device_id_type=MESH)
     pl.semaphore_signal(barrier, inc=1, device_id=(prv, me), device_id_type=MESH)
+    relayed = [d for d in range(2, parts, 2) if d >= parts - parts // 4]
+    for d in relayed:
+        for neighbour in (nxt, prv):
+            pl.semaphore_signal(
+                barrier, inc=1, device_id=(neighbour, flipped(me, d)), device_id_type=MESH
+            )
     for a in range(adapters):
         down32[a * rank_share : (a + 1) * rank_share, :] = down_ref[0, a].astype(F32)
     xbuf[0, 0] = x_ref[0]
-    pl.semaphore_wait(barrier, parts + 1)
+    pl.semaphore_wait(barrier, parts + 1 + 2 * len(relayed))
 
     def send(src, dst, ssem, rsem, device):
         copy = pltpu.make_async_remote_copy(
@@ -120,7 +126,6 @@
         return copy
 
     far_first = list(range(parts - 1, 0, -1))
-    relayed = [d for d in range(2, parts, 2) if d >= parts - parts // 4]
     via_partner = [d + 1 for d in relayed]
     direct = [d for d in far_first if d not in via_partner]
     near = [d for d in range(2, parts) if d not in relayed and d not in via_partner]
@@ -128,10 +133,14 @@
     arrival = [0, 1] + relayed + near + via_partner
     partner = flipped(me, 1)
     pending = []
+    x_ahead = {}
 
     def spread_x(t, src):
         copies = [None] * parts
         for d in direct:
+            if t > 0 and d in relayed:
+                copies[d] = x_ahead[d]
+                continue
             copies[d] = send(
                 src, xbuf.at[t, d], x_send.at[t, d], x_recv.at[t, d], (section, flipped(me, d))
             )
@@ -384,6 +393,14 @@
                 out_ref.at[0, t], xbuf.at[t + 1, 0], z_send.at[t], z_recv.at[t], (nxt, me)
             )
             pending.append(z_copy)
+            for d in relayed:
+                x_ahead[d] = send(
+                    out_ref.at[0, t],
+                    xbuf.at[t + 1, d],
+                    x_send.at[t + 1, d],
+                    x_recv.at[t + 1, d],
+                    (nxt, flipped(me, d)),
+                )
 
     for copy in pending:
         copy.wait_send()

time: 59.3 us -> 57.9 us (0.976)
  Pallas kernels: 57.6 us -> 56.2 us
    pallas_call x1, Pallas kernels: 57.6 us -> 56.2 us  [local(): pl.pallas_call(functools.partial(kernel, sections, parts), out_shape=jax....]
where the time goes in v4:
time: 57.9 us; the launch traced here: 57.8 us
  Pallas kernels  56.2 us (97%)
  local copies, waits for them, and re-layouts  1.54 us (3%)
    pallas_call x1, Pallas kernels, local(): pl.pallas_call(functools.partial(kernel, sections, parts), out_shape=jax....  56.2 us
    unnamed x1, local copies, waits for them, and re-layouts  1.54 us

profile of v4, /device:TPU:0, one launch (start us, length us, event | category | flops | bytes accessed | tf_op | source)
XLA Modules:
  0.0 57.8 jit_solution(552949874792886850)
XLA Ops:
  0.0 56.2 %shard_map.91 = bf16[1,3,16,1024]{3,2,1,0:T(8,128)(2,1)} custom-call(s32[4,16]{1,0:T(4,128)} %adapter_ref.1, s32[4,16]{1,0:T(4,128)} %lens_ref.1, bf16[1,16,1024]{2,1,0:T(8,128)(2,1)} %x_ref.1, bf16[1,8192]{1,0:T(2,128)(2,1)} %gain_ref.1, bf16[1,8192,512]{2,1,0:T(8,128)(2,1)} %wq_hbm.1, bf16[1,512,8192]{2,1,0:T(8,128)(2,1)} %wo_hbm.1, ...), custom_call_target="tpu_custom_call" | custom-call | tf_op jit(solution)/shard_map/pallas_call | solution.py:431
  56.2 1.5 %copy.11 = bf16[1,3,16,1024]{3,2,1,0:T(8,128)(2,1)} copy(bf16[1,3,16,1024]{3,2,1,0:T(8,128)(2,1)} %shard_map.91) | data formatting | bytes 196608
